TPU v7x, 32 devices: a whole 2x2x4 slice. The times are simulated.
32 devices in a mesh: tile: 8 (over z, core), layer: 4 (over y, x).
Axes of the slice: x: 2, y: 2, z: 4, core: 2. Of those that a mesh axis runs over, the one named last changes fastest.
Arguments:
- basis: float32 [8, 768, 32], P('tile'), may hold values from -0.21875 to 0.21875
- ranks: int32 [8], P('tile'), may hold values from 8 to 32
- cores: float32 [8, 8, 32, 32], P('tile', 'layer'), may hold values from -1.11 to 1.11
- diag: float32 [8, 768, 768], P('tile', 'layer'), may hold values from 0 to 9, as said below
Outputs:
- factors: float32 [1, 768, 768], P(None, 'layer')
- panel_basis: float32 [1, 768, 32], replicated
- schur_diag: float32 [8, 768, 768], P('tile', 'layer')
- schur_cores: float32 [8, 8, 32, 32], P('tile', 'layer')
Inputs may be any that keep to these rules, and one draw needn't show every extreme that they name: `diag`: each tile is a Gaussian kernel of points in the unit cube plus a multiple of the identity, so symmetric positive definite.
All inputs are finite; a program needn't handle non-finite values.
Results may differ from a plain program's by a relative error of at most 0.0001.
Values sent between devices are 32-bit elements; how exact they have to be, the bound alone decides.
A program may use at most 64 MiB of HBM per device.

v0:
```python
import functools

import jax
import jax.numpy as jnp
from jax import lax
from jax.experimental import pallas as pl
from jax.experimental.pallas import tpu as pltpu
from jax.sharding import PartitionSpec as P

B = 128
S = 8
NEAR = 2


def split(a):
    high = a.astype(jnp.bfloat16)
    return high, (a - high.astype(jnp.float32)).astype(jnp.bfloat16)


def three(a, b, dims):
    ah, al = split(a)
    bh, bl = split(b)
    dot = functools.partial(
        lax.dot_general, dimension_numbers=(dims, ((), ())), preferred_element_type=jnp.float32
    )
    return dot(ah, bh) + (dot(ah, bl) + dot(al, bh))


def nt(a, b):
    return three(a, b, ((1,), (1,)))


def nn(a, b):
    return three(a, b, ((1,), (0,)))


def total(terms):
    while len(terms) > 1:
        terms = [
            terms[i] + terms[i + 1] if i + 1 < len(terms) else terms[i]
            for i in range(0, len(terms), 2)
        ]
    return terms[0]


def spread_lane(block, lane):
    return jnp.broadcast_to(block[:, lane : lane + 1], (S, B))


def pick_lane(block, lane):
    return jnp.take_along_axis(block, jnp.full((S, B), lane, jnp.int32), axis=1)


def spread_row(block, row):
    return jnp.broadcast_to(block[row : row + 1, :], (S, B))


def base_factor(tile_ref, upper_ref, inv_ref):
    groups = B // S
    sub = lax.broadcasted_iota(jnp.int32, (S, B), 0)
    lane = lax.broadcasted_iota(jnp.int32, (S, B), 1)
    left = [tile_ref[S * g : S * g + S, :] for g in range(groups)]
    for b in range(groups):
        a = left[b]
        q = jnp.where(lane < S * b, a, jnp.where(lane == sub + S * b, 1.0, 0.0))
        cols = [pick_lane(a, S * b + j) for j in range(S)]
        e = [[spread_row(cols[j], i) if j <= i else None for j in range(S)] for i in range(S)]
        inv, low = [], [[None] * S for _ in range(S)]
        for j in range(S):
            inv.append(1.0 / e[j][j])
            for i in range(j + 1, S):
                low[i][j] = e[i][j] * inv[j]
            for k in range(j + 1, S):
                for i in range(k, S):
                    e[i][k] = e[i][k] - low[i][j] * e[k][j]
        ra = [spread_row(a, i) for i in range(S)]
        rq = [spread_row(q, i) for i in range(S)]
        for j in range(S):
            for i in range(j + 1, S):
                ra[i] = ra[i] - low[i][j] * ra[j]
                rq[i] = rq[i] - low[i][j] * rq[j]
        xa, xq = None, None
        for j in range(S):
            root = lax.rsqrt(e[j][j])
            ya, yq = ra[j] * root, rq[j] * root
            xa = ya if xa is None else jnp.where(sub == j, ya, xa)
            xq = yq if xq is None else jnp.where(sub == j, yq, xq)
        upper_ref[S * b : S * b + S, :] = jnp.where(lane >= sub + S * b, xa, 0.0)
        inv_ref[S * b : S * b + S, :] = xq
        if b + 1 == groups:
            break
        done = lane < S * b + S
        w = [jnp.where(done, rq[j], ra[j]) * inv[j] for j in range(S)]
        for i in range(S - 1, 0, -1):
            for j in range(i):
                w[j] = w[j] - low[i][j] * w[i]
        pivots = done & (lane >= S * b)
        for g in range(b + 1, min(b + 1 + NEAR, groups)):
            m = [spread_lane(left[g], S * b + j) for j in range(S)]
            left[g] = jnp.where(pivots, 0.0, left[g]) - total([m[j] * w[j] for j in range(S)])
        far = b + 1 + NEAR
        if far < groups:
            packed = w[0]
            for j in range(1, S):
                packed = jnp.where(sub == j, w[j], packed)
            rows = [packed if g == b else jnp.zeros((S, B), jnp.float32) for g in range(groups)]
            moved = nn(jnp.concatenate(left[far:], axis=0), jnp.concatenate(rows, axis=0))
            for g in range(far, groups):
                at = S * (g - far)
                left[g] = jnp.where(pivots, 0.0, left[g]) - moved[at : at + S, :]


def panel_kernel(
    tiles, layers, diag_ref, masked_t_ref, cores_ref,
    factor_ref, z_ref, diag_out, cores_out,
    work, zt, low, block, upper, inverse, col, oth,
    ztv, own_rows, send1, recv1, send2, recv2, sendu, recvu, sendc, recvc, sendo, recvo,
):
    t = lax.axis_index("tile")
    l = lax.axis_index("layer")
    rows, order = diag_ref.shape[1], diag_ref.shape[2]
    panels = order // B
    span = cores_ref.shape[1]
    pair_base = t - t % 2
    mine = pl.ds(pl.multiple_of(l * rows, S), rows)
    first = t == 0
    even = t % 2 == 0

    def needed(j, piece):
        return (piece + 1) * rows > j * B

    def remote(src, dst, send, recv, to_t, to_l):
        return pltpu.make_async_remote_copy(
            src_ref=src, dst_ref=dst, send_sem=send, recv_sem=recv,
            device_id=(to_t, to_l), device_id_type=pl.DeviceIdType.MESH,
        )

    def down(j, half):
        return remote(
            diag_ref.at[0, :, pl.ds(pl.multiple_of(j * B, B), B)], work.at[j, mine, :],
            send1.at[half, j], recv1.at[j], 2 * half, l,
        )

    def kept(j):
        return pltpu.make_async_copy(
            diag_ref.at[0, :, pl.ds(pl.multiple_of(j * B, B), B)], work.at[j, mine, :], recv1.at[j]
        )

    def across(j, core, to_l):
        slot = work.at[j, mine, :]
        return remote(slot, slot, send2.at[j, core, to_l], recv2.at[j, l], pair_base + core, to_l)

    def landed(j, piece):
        slot = work.at[j, pl.ds(pl.multiple_of(piece * rows, S), rows), :]
        return remote(slot, slot, send2.at[j, 0, 0], recv2.at[j, piece], t, l)

    def basis_down(half):
        return remote(masked_t_ref, zt, sendu.at[half], recvu, 2 * half, l)

    def basis_kept():
        return pltpu.make_async_copy(masked_t_ref, zt, recvu)

    def basis_across():
        return remote(zt, zt, sendu.at[0], recvu, t + 1, l)

    def column_to(to_l):
        return remote(cores_ref.at[0, 0], col, sendc.at[to_l], recvc, t, to_l)

    def other_to(to_t):
        return remote(
            cores_ref.at[0, 0], oth.at[t % span], sendo.at[to_t], recvo.at[t % span], to_t, t // span
        )

    def each(count, act):
        lax.fori_loop(0, count, lambda i, c: (act(i), c)[1], 0)

    barrier = pltpu.get_barrier_semaphore()
    devices = tiles * layers
    me = t * layers + l

    def greet(i):
        d = lax.rem(me + 1 + i, devices)
        pl.semaphore_signal(
            barrier, inc=1, device_id=(d // layers, d % layers),
            device_id_type=pl.DeviceIdType.MESH,
        )

    @pl.when(first)
    def _():
        each(panels, lambda j: pl.when(needed(j, l))(lambda: kept(j).start()))
        basis_kept().start()

    each(devices - 1, greet)
    pl.semaphore_wait(barrier, devices - 1)

    def relay(j):
        @pl.when(even & needed(j, l))
        def _():
            @pl.when(first)
            def _():
                kept(j).wait()

            @pl.when(jnp.logical_not(first))
            def _():
                down(j, 0).wait_recv()

            def send(i):
                to_l = lax.rem(l + 1 + i, layers)
                across(j, 0, to_l).start()
                across(j, 1, to_l).start()

            across(j, 1, l).start()
            each(layers - 1, send)

    def arrive(j):
        def take(piece):
            @pl.when(needed(j, piece) & (jnp.logical_not(even) | (piece != l)))
            def _():
                landed(j, piece).wait_recv()

        each(layers, take)

    @pl.when(first)
    def _():
        def chunk(j):
            pl.when(needed(j, l))(
                lambda: each(tiles // 2 - 1, lambda h: down(j, tiles // 2 - 1 - h).start())
            )

        chunk(0)
        if panels > 1:
            chunk(1)
        each(tiles // 2 - 1, lambda h: basis_down(tiles // 2 - 1 - h).start())
        each(panels - 2, lambda j: chunk(j + 2))

    relay(0)

    @pl.when(l == 0)
    def _():
        each(layers - 1, lambda i: column_to(i + 1).start())
        pltpu.make_async_copy(cores_ref.at[0, 0], col, recvc).start()

        def other(i):
            to_t = lax.rem(t + i, tiles)

            @pl.when((to_t != t) | (t // span != 0))
            def _():
                other_to(to_t).start()

        each(tiles, other)

        @pl.when(t // span == 0)
        def _():
            pltpu.make_async_copy(cores_ref.at[0, 0], oth.at[t % span], recvo.at[t % span]).start()

    def basis_relay():
        @pl.when(first)
        def _():
            basis_kept().wait()

        @pl.when(jnp.logical_not(first))
        def _():
            basis_down(0).wait_recv()

        @pl.when(even)
        def _():
            basis_across().start()

    low[...] = jnp.zeros_like(low)
    own_rows[...] = masked_t_ref[...].T

    def panel(k, carry):
        at = pl.ds(pl.multiple_of(k * B, B), B)
        arrive(k)

        @pl.when(k + 1 < panels)
        def _():
            relay(k + 1)

        for c in range(panels):
            @pl.when(k == c)
            def _():
                here = slice(c * B, c * B + B)
                if c:
                    work2 = work[c, c * B :, :] - nt(low[c * B :, : c * B], low[here, : c * B])
                    low[c * B :, here] = work2
                else:
                    low[:, here] = work[0]
        block[...] = low[at, at]

        base_factor(block, upper, inverse)
        low[at, at] = upper[...].T

        @pl.when(k == 0)
        def _():
            basis_relay()
            ztv[...] = zt[...]

        for c in range(panels):
            @pl.when(k == c)
            def _():
                here = slice(c * B, c * B + B)
                rest = slice(c * B + B, order)
                part = ztv[:, here]
                if c:
                    part = part - nt(ztv[:, : c * B], low[here, : c * B])
                ztv[:, here] = nt(part, inverse[...])
                if c + 1 < panels:
                    low[rest, here] = nt(low[rest, here], inverse[...])
        return carry

    lax.fori_loop(0, panels, panel, 0)

    factor_ref[0] = low[mine, :]
    z_ref[...] = ztv[...]
    gram = nt(ztv[...], ztv[...])

    @pl.when(l == 0)
    def _():
        pltpu.make_async_copy(cores_ref.at[0, 0], col, recvc).wait()

    @pl.when(l != 0)
    def _():
        column_to(0).wait_recv()

    def take_other(s):
        local = (l == 0) & (l * span + s == t)

        @pl.when(local)
        def _():
            pltpu.make_async_copy(cores_ref.at[0, 0], oth.at[s], recvo.at[s]).wait()

        @pl.when(jnp.logical_not(local))
        def _():
            remote(cores_ref.at[0, 0], oth.at[s], sendo.at[0], recvo.at[s], t, l).wait_recv()

    each(span, take_other)
    coef = nn(col[...], gram)
    inner = nt(coef, col[...])
    inner = jnp.where(t > 0, inner, 0.0)
    partial = nn(own_rows[mine, :], inner)
    diag_out[0] = diag_ref[0] - nn(partial, masked_t_ref[...])
    for s in range(span):
        other_id = l * span + s
        live = (t > other_id) & (other_id > 0)
        cores_out[0, s] = cores_ref[0, s] - jnp.where(live, nt(coef, oth[s]), 0.0)

    @pl.when(first)
    def _():
        def chunk(j):
            pl.when(needed(j, l))(lambda: each(tiles // 2 - 1, lambda h: down(j, h + 1).wait_send()))

        each(panels, chunk)
        each(tiles // 2 - 1, lambda h: basis_down(h + 1).wait_send())

    @pl.when(even)
    def _():
        basis_across().wait_send()

        def chunk(j):
            @pl.when(needed(j, l))
            def _():
                across(j, 1, l).wait_send()

                def sent(i):
                    to_l = lax.rem(l + 1 + i, layers)
                    across(j, 0, to_l).wait_send()
                    across(j, 1, to_l).wait_send()

                each(layers - 1, sent)

        each(panels, chunk)

    @pl.when(l == 0)
    def _():
        each(layers - 1, lambda i: column_to(i + 1).wait_send())

        def other(i):
            to_t = lax.rem(t + i, tiles)

            @pl.when((to_t != t) | (t // span != 0))
            def _():
                other_to(to_t).wait_send()

        each(tiles, other)


def body(tiles, layers, basis, ranks, cores, diag):
    rmax = basis.shape[2]
    span = cores.shape[1]
    rows, order = diag.shape[1], diag.shape[2]
    panels = order // B
    keep = (jnp.arange(rmax, dtype=jnp.int32)[None, :] < ranks[:, None]).astype(jnp.float32)
    masked = basis * keep[:, None, :]
    masked_t = masked[0].T
    vm = pl.BlockSpec(memory_space=pltpu.VMEM)
    f32 = jnp.float32
    dma = pltpu.SemaphoreType.DMA
    factors, zt, schur, couplings = pl.pallas_call(
        functools.partial(panel_kernel, tiles, layers),
        out_shape=(
            jax.ShapeDtypeStruct((1, rows, order), f32),
            jax.ShapeDtypeStruct((rmax, order), f32),
            jax.ShapeDtypeStruct(diag.shape, f32),
            jax.ShapeDtypeStruct(cores.shape, f32),
        ),
        in_specs=[vm] * 3,
        out_specs=(vm,) * 4,
        scratch_shapes=[
            pltpu.VMEM((panels, order, B), f32),
            pltpu.VMEM((rmax, order), f32),
            pltpu.VMEM((order, order), f32),
            pltpu.VMEM((B, B), f32),
            pltpu.VMEM((B, B), f32),
            pltpu.VMEM((B, B), f32),
            pltpu.VMEM((rmax, rmax), f32),
            pltpu.VMEM((span, rmax, rmax), f32),
            pltpu.VMEM((rmax, order), f32),
            pltpu.VMEM((order, rmax), f32),
            dma((tiles // 2, panels)),
            dma((panels,)),
            dma((panels, 2, layers)),
            dma((panels, layers)),
            dma((tiles // 2,)),
            dma,
            dma((layers,)),
            dma,
            dma((tiles,)),
            dma((span,)),
        ],
        compiler_params=pltpu.CompilerParams(collective_id=0, has_side_effects=True),
    )(diag, masked_t, cores)
    return factors, zt.T[None], schur, couplings


def solution(mesh):
    placed = (
        P("tile", None, None),
        P("tile"),
        P("tile", "layer", None, None),
        P("tile", "layer", None),
    )
    return jax.shard_map(
        functools.partial(body, mesh.shape["tile"], mesh.shape["layer"]),
        mesh=mesh,
        in_specs=placed,
        out_specs=(
            P(None, "layer", None),
            P(),
            P("tile", "layer", None),
            P("tile", "layer", None, None),
        ),
        check_vma=False,
    )
```

profile of v0, /device:TPU:11, one launch (start us, length us, event | category | flops | bytes accessed | tf_op | source)
XLA Modules:
  0.0 59.3 jit_solution(18312934246080715421)
XLA Ops:
  1.3 1.6 %multiply_bitcast_fusion.masked_t_ref = f32[32,768]{1,0:T(8,128)} fusion(f32[1,768,32]{1,2,0:T(8,128)} %param.4, f32[32]{0:T(128)S(1)} %compare_convert_fusion), kind=kLoop, calls=%fused_computation | loop fusion | flops 24576 | bytes 196736 | tf_op jit(solution)/shard_map/transpose | solution.py:395
  2.9 52.3 %shard_map.75 = (f32[1,192,768]{2,1,0:T(8,128)}, f32[32,768]{1,0:T(8,128)}, f32[1,192,768]{2,1,0:T(8,128)}, f32[1,2,32,32]{3,2,1,0:T(8,128)}) custom-call(f32[1,192,768]{2,1,0:T(8,128)} %diag_ref.1, f32[32,768]{1,0:T(8,128)} %multiply_bitcast_fusion.masked_t_ref, f32[1,2,32,32]{3,2,1,0:T(8,128)} %cores_ref.1), custom_call_target="tpu_custom_call" | custom-call | tf_op jit(solution)/shard_map/pallas_call | solution.py:399
  55.2 0.0 copy-start.1
  55.2 0.0 copy-start
  55.2 2.0 %copy.13 = f32[1,192,768]{2,1,0:T(8,128)} copy(f32[1,192,768]{2,1,0:T(8,128)} %get-tuple-element.16) | data formatting | bytes 1179648
  57.2 0.0 copy-done.1
  57.2 0.6 %copy.14 = f32[1,768,32]{1,2,0:T(8,128)} copy(f32[1,768,32]{1,2,0:T(8,128)S(1)} %bitcast.9) | data formatting | bytes 196608
  57.8 0.0 copy-done
  57.8 0.0 copy-start.2
  57.8 0.8 %copy.15 = f32[1,192,768]{2,1,0:T(8,128)} copy(f32[1,192,768]{2,1,0:T(8,128)S(1)} %copy-done) | data formatting | bytes 1179648
  58.7 0.0 copy-done.2
  58.7 0.6 %copy.16 = f32[1,2,32,32]{3,2,1,0:T(8,128)} copy(f32[1,2,32,32]{3,2,1,0:T(8,128)S(1)} %copy-done.2) | data formatting | bytes 16384
  (1 shorter events, 0.0 us)
Async XLA Ops:
  55.2 2.0 %copy-start.1 = (f32[32,768]{1,0:T(8,128)S(1)}, f32[32,768]{1,0:T(8,128)}, u32[]{:S(2)}) copy-start(f32[32,768]{1,0:T(8,128)} %get-tuple-element.9) | copy-start | bytes 294916
  55.2 2.6 %copy-start = (f32[1,192,768]{2,1,0:T(8,128)S(1)}, f32[1,192,768]{2,1,0:T(8,128)}, u32[]{:S(2)}) copy-start(f32[1,192,768]{2,1,0:T(8,128)} %get-tuple-element.18) | copy-start | bytes 1769476
  57.8 0.8 %copy-start.2 = (f32[1,2,32,32]{3,2,1,0:T(8,128)S(1)}, f32[1,2,32,32]{3,2,1,0:T(8,128)}, u32[]{:S(2)}) copy-start(f32[1,2,32,32]{3,2,1,0:T(8,128)} %get-tuple-element.19) | copy-start | bytes 24580
where the time goes:
time: 59.5 us; the launch traced here: 59.3 us
  Pallas kernels  52.3 us (88%)
  local copies, waits for them, and re-layouts  4.07 us (7%)
  other arithmetic  1.61 us (3%)
  between operations  1.31 us (2%)
    pallas_call x1, Pallas kernels, body(): pl.pallas_call(functools.partial(panel_kernel, tiles, layers), out_shape=...  52.3 us
    unnamed x10, local copies, waits for them, and re-layouts  4.07 us
    transpose x1, other arithmetic, body(): masked_t = masked[0].T  1.61 us

commit v1 on v0

v1 whole, which is shorter than its diff:
```python
import functools

import jax
import jax.numpy as jnp
from jax import lax
from jax.experimental import pallas as pl
from jax.experimental.pallas import tpu as pltpu
from jax.sharding import PartitionSpec as P

B = 128
S = 8
NEAR = 2


def split(a):
    high = a.astype(jnp.bfloat16)
    return high, (a - high.astype(jnp.float32)).astype(jnp.bfloat16)


def three(a, b, dims):
    ah, al = split(a)
    bh, bl = split(b)
    dot = functools.partial(
        lax.dot_general, dimension_numbers=(dims, ((), ())), preferred_element_type=jnp.float32
    )
    return dot(ah, bh) + (dot(ah, bl) + dot(al, bh))


def nt(a, b):
    return three(a, b, ((1,), (1,)))


def nn(a, b):
    return three(a, b, ((1,), (0,)))


def tn(a, b):
    return three(a, b, ((0,), (0,)))


def total(terms):
    while len(terms) > 1:
        terms = [
            terms[i] + terms[i + 1] if i + 1 < len(terms) else terms[i]
            for i in range(0, len(terms), 2)
        ]
    return terms[0]


def spread_lane(block, lane):
    return jnp.broadcast_to(block[:, lane : lane + 1], (S, B))


def pick_lane(block, lane):
    return jnp.take_along_axis(block, jnp.full((S, B), lane, jnp.int32), axis=1)


def spread_row(block, row):
    return jnp.broadcast_to(block[row : row + 1, :], (S, B))


def base_factor(tile_ref, upper_ref, inv_ref):
    groups = B // S
    sub = lax.broadcasted_iota(jnp.int32, (S, B), 0)
    lane = lax.broadcasted_iota(jnp.int32, (S, B), 1)
    left = [tile_ref[S * g : S * g + S, :] for g in range(groups)]
    for b in range(groups):
        a = left[b]
        q = jnp.where(lane < S * b, a, jnp.where(lane == sub + S * b, 1.0, 0.0))
        cols = [pick_lane(a, S * b + j) for j in range(S)]
        e = [[spread_row(cols[j], i) if j <= i else None for j in range(S)] for i in range(S)]
        inv, low = [], [[None] * S for _ in range(S)]
        for j in range(S):
            inv.append(1.0 / e[j][j])
            for i in range(j + 1, S):
                low[i][j] = e[i][j] * inv[j]
            for k in range(j + 1, S):
                for i in range(k, S):
                    e[i][k] = e[i][k] - low[i][j] * e[k][j]
        ra = [spread_row(a, i) for i in range(S)]
        rq = [spread_row(q, i) for i in range(S)]
        for j in range(S):
            for i in range(j + 1, S):
                ra[i] = ra[i] - low[i][j] * ra[j]
                rq[i] = rq[i] - low[i][j] * rq[j]
        xa, xq = None, None
        for j in range(S):
            root = lax.rsqrt(e[j][j])
            ya, yq = ra[j] * root, rq[j] * root
            xa = ya if xa is None else jnp.where(sub == j, ya, xa)
            xq = yq if xq is None else jnp.where(sub == j, yq, xq)
        upper_ref[S * b : S * b + S, :] = jnp.where(lane >= sub + S * b, xa, 0.0)
        inv_ref[S * b : S * b + S, :] = xq
        if b + 1 == groups:
            break
        done = lane < S * b + S
        w = [jnp.where(done, rq[j], ra[j]) * inv[j] for j in range(S)]
        for i in range(S - 1, 0, -1):
            for j in range(i):
                w[j] = w[j] - low[i][j] * w[i]
        pivots = done & (lane >= S * b)
        for g in range(b + 1, min(b + 1 + NEAR, groups)):
            m = [spread_lane(left[g], S * b + j) for j in range(S)]
            left[g] = jnp.where(pivots, 0.0, left[g]) - total([m[j] * w[j] for j in range(S)])
        far = b + 1 + NEAR
        if far < groups:
            packed = w[0]
            for j in range(1, S):
                packed = jnp.where(sub == j, w[j], packed)
            rows = [packed if g == b else jnp.zeros((S, B), jnp.float32) for g in range(groups)]
            moved = nn(jnp.concatenate(left[far:], axis=0), jnp.concatenate(rows, axis=0))
            for g in range(far, groups):
                at = S * (g - far)
                left[g] = jnp.where(pivots, 0.0, left[g]) - moved[at : at + S, :]


def panel_kernel(
    tiles, layers, diag_ref, basis_ref, ranks_ref, cores_ref,
    factor_ref, z_ref, diag_out, cores_out,
    work, low, block, upper, inverse, masked_t, col, oth, w_rows, w_cols, gram,
    local, recv_work, send_work, recv_low, send_low, recv_z, send_z,
    recvc, sendc, recvo, sendo,
):
    t = lax.axis_index("tile")
    l = lax.axis_index("layer")
    rows, order = diag_ref.shape[1], diag_ref.shape[2]
    rmax = basis_ref.shape[0]
    panels = order // B
    early = order - B
    span = cores_ref.shape[1]
    half = tiles // 2
    hub = (t == 0) & (l == 0)
    spoke = jnp.logical_not(hub)
    fan = ((t == 0) & (l > 0)) | ((t == 1) & (l == 0))
    side = (t % 2 == 0) & spoke

    def remote(src, dst, send, recv, to_t, to_l):
        return pltpu.make_async_remote_copy(
            src_ref=src, dst_ref=dst, send_sem=send, recv_sem=recv,
            device_id=(to_t, to_l), device_id_type=pl.DeviceIdType.MESH,
        )

    def each(count, act):
        lax.fori_loop(0, count, lambda i, c: (act(i), c)[1], 0)

    def needed(j, piece):
        return (piece + 1) * rows > j * B

    def columns(j):
        return pl.ds(pl.multiple_of(j * B, B), B)

    def slot(j, piece):
        return work.at[j, pl.ds(pl.multiple_of(piece * rows, S), rows), :]

    def gathered(j):
        return remote(
            diag_ref.at[0, :, columns(j)], slot(j, l), send_work.at[j], recv_work.at[j, l], 0, 0
        )

    def kept(j):
        return pltpu.make_async_copy(
            diag_ref.at[0, :, columns(j)], slot(j, 0), recv_work.at[j, 0]
        )

    def landed(j, piece):
        return remote(slot(j, piece), slot(j, piece), send_work.at[j], recv_work.at[j, piece], t, l)

    def parts(k):
        whole, cut = (k * B) // rows, (k * B) % rows
        if cut:
            return [(l == whole, whole, whole + 1, cut), (l > whole, whole + 1, layers, 0)]
        return [(l >= whole, whole, layers, 0)]

    def down_low(k, at, to_t, child):
        piece = factor_ref.at[0, at:, k * B : k * B + B]
        return remote(piece, piece, send_low.at[k, child], recv_low.at[k], to_t, l)

    def out_low(k, at, piece):
        return remote(
            low.at[pl.ds(pl.multiple_of(piece * rows + at, S), rows - at), k * B : k * B + B],
            factor_ref.at[0, at:, k * B : k * B + B],
            send_low.at[k, piece], recv_low.at[k], jnp.where(piece == 0, 1, 0), piece,
        )

    def out_z(part, piece):
        cut = z_ref.at[:, early:] if part else z_ref.at[:, :early]
        return remote(
            cut, cut, send_z.at[part, piece], recv_z.at[part], jnp.where(piece == 0, 1, 0), piece
        )

    def down_z(part, to_t, child):
        cut = z_ref.at[:, early:] if part else z_ref.at[:, :early]
        return remote(cut, cut, send_z.at[part, child], recv_z.at[part], to_t, l)

    def onward(copy, act):
        @pl.when(fan)
        def _():
            each(half - 1, lambda i: act(copy(2 * (half - 1 - i), half - 1 - i)))

        @pl.when(side)
        def _():
            act(copy(t + 1, 0))

    def start(copy):
        copy.start()

    def sent(copy):
        copy.wait_send()

    def column_to(to_l):
        return remote(cores_ref.at[0, 0], col, sendc.at[to_l], recvc, t, to_l)

    def column_kept():
        return pltpu.make_async_copy(cores_ref.at[0, 0], col, recvc)

    def other_to(to_t):
        return remote(
            cores_ref.at[0, 0], oth.at[t % span], sendo.at[to_t], recvo.at[t % span], to_t, t // span
        )

    def other_kept():
        return pltpu.make_async_copy(cores_ref.at[0, 0], oth.at[t % span], recvo.at[t % span])

    basis_in = pltpu.make_async_copy(basis_ref, masked_t, local.at[0])
    diag_in = pltpu.make_async_copy(diag_ref, diag_out, local.at[1])
    cores_in = pltpu.make_async_copy(cores_ref, cores_out, local.at[2])

    def mask():
        basis_in.wait()
        row = lax.broadcasted_iota(jnp.int32, (rmax, order), 0)
        masked_t[...] = masked_t[...] * jnp.where(row < ranks_ref[0], 1.0, 0.0)

    barrier = pltpu.get_barrier_semaphore()
    devices = tiles * layers

    @pl.when(hub)
    def _():
        each(panels, lambda j: pl.when(needed(j, 0))(lambda: kept(j).start()))
        basis_in.start()

        def greet(i):
            pl.semaphore_signal(
                barrier, inc=1, device_id=((i + 1) // layers, (i + 1) % layers),
                device_id_type=pl.DeviceIdType.MESH,
            )

        each(devices - 1, greet)

    @pl.when(spoke)
    def _():
        factor_ref[...] = jnp.zeros_like(factor_ref)
        pl.semaphore_signal(barrier, inc=1, device_id=(0, 0), device_id_type=pl.DeviceIdType.MESH)
        pl.semaphore_wait(barrier, 1)

    def gather(j):
        if 0 < j <= panels:
            pl.when((t == 0) & spoke & needed(j - 1, l))(lambda: gathered(j - 1).wait_send())
        if j < panels:
            pl.when((t == 0) & spoke & needed(j, l))(lambda: gathered(j).start())

    for j in range(3):
        gather(j)

    diag_in.start()
    cores_in.start()

    @pl.when(hub)
    def _():
        low[...] = jnp.zeros_like(low)

        def panel(k, carry):
            at = pl.ds(pl.multiple_of(k * B, B), B)

            @pl.when(needed(k, 0))
            def _():
                kept(k).wait()

            def take(piece):
                pl.when(needed(k, piece + 1))(lambda: landed(k, piece + 1).wait_recv())

            each(layers - 1, take)

            for c in range(panels):
                @pl.when(k == c)
                def _():
                    here = slice(c * B, c * B + B)
                    if c:
                        work2 = work[c, c * B :, :] - nt(low[c * B :, : c * B], low[here, : c * B])
                        low[c * B :, here] = work2
                    else:
                        low[:, here] = work[0]
            block[...] = low[at, at]

            base_factor(block, upper, inverse)
            low[at, at] = upper[...].T

            @pl.when(k == 0)
            def _():
                mask()
                pl.semaphore_wait(barrier, devices - 1)

            for c in range(panels):
                @pl.when(k == c)
                def _():
                    here = slice(c * B, c * B + B)
                    rest = slice(c * B + B, order)
                    if c + 1 < panels:
                        low[rest, here] = nt(low[rest, here], inverse[...])
                    part = masked_t[:, here]
                    if c:
                        part = part - nt(z_ref[:, : c * B], low[here, : c * B])
                    z_ref[:, here] = nt(part, inverse[...])
                    if c == panels - 1:
                        each(layers, lambda piece: out_z(1, piece).start())
                    for _, first, last, cut in parts(c):
                        each(last - first, lambda i: out_low(c, cut, first + i).start())
                    if c == panels - 2:
                        each(layers, lambda piece: out_z(0, piece).start())
            return carry

        lax.fori_loop(0, panels, panel, 0)
        factor_ref[0] = low[:rows, :]

    @pl.when(spoke)
    def _():
        basis_in.start()

        def relay(k):
            for mine, _, _, cut in parts(k):
                @pl.when(mine)
                def _():
                    down_low(k, cut, t, 0).wait_recv()
                    onward(lambda to_t, child: down_low(k, cut, to_t, child), start)

            gather(k + 3)

        relay(0)

        @pl.when(t > 0)
        def _():
            @pl.when(l == 0)
            def _():
                each(layers - 1, lambda i: column_to(i + 1).start())
                column_kept().start()

                def other(i):
                    to_t = 1 + lax.rem(t - 1 + i, tiles - 1)
                    pl.when((to_t != t) | (t // span != 0))(lambda: other_to(to_t).start())

                each(tiles - 1, other)
                pl.when(t // span == 0)(lambda: other_kept().start())

        relay(1)

        @pl.when(t > 0)
        def _():
            pl.when(l == 0)(lambda: column_kept().wait())
            pl.when(l != 0)(lambda: column_to(0).wait_recv())

            def take_other(s):
                mine = (l == 0) & (l * span + s == t)

                @pl.when(mine)
                def _():
                    pltpu.make_async_copy(cores_ref.at[0, 0], oth.at[s], recvo.at[s]).wait()

                @pl.when(jnp.logical_not(mine) & (l * span + s > 0))
                def _():
                    remote(cores_ref.at[0, 0], oth.at[s], sendo.at[0], recvo.at[s], t, l).wait_recv()

            each(span, take_other)
            mask()
            w_cols[...] = tn(col[...], masked_t[...])
            own = masked_t[...].T
            w_rows[...] = nn(own, col[...])

        for k in range(2, panels - 1):
            relay(k)
        down_z(0, t, 0).wait_recv()
        onward(lambda to_t, child: down_z(0, to_t, child), start)
        gram[...] = nt(z_ref[:, :early], z_ref[:, :early])
        down_z(1, t, 0).wait_recv()
        onward(lambda to_t, child: down_z(1, to_t, child), start)
        relay(panels - 1)

        @pl.when(t == 0)
        def _():
            basis_in.wait()

    diag_in.wait()
    cores_in.wait()

    @pl.when(t > 0)
    def _():
        mine = pl.ds(pl.multiple_of(l * rows, S), rows)
        square = gram[...] + nt(z_ref[:, early:], z_ref[:, early:])
        partial = nn(w_rows[mine, :], square)
        diag_out[0] = diag_out[0] - nn(partial, w_cols[...])
        coef = nn(col[...], square)
        for s in range(span):
            other_id = l * span + s

            @pl.when((t > other_id) & (other_id > 0))
            def _():
                cores_out[0, s] = cores_out[0, s] - nt(coef, oth[s])

    @pl.when(hub)
    def _():
        for c in range(panels):
            for _, first, last, cut in parts(c):
                each(last - first, lambda i: out_low(c, cut, first + i).wait_send())
        for part in range(2):
            each(layers, lambda piece: out_z(part, piece).wait_send())

    @pl.when(spoke)
    def _():
        for k in range(panels):
            for mine, _, _, cut in parts(k):
                @pl.when(mine)
                def _():
                    onward(lambda to_t, child: down_low(k, cut, to_t, child), sent)
        for part in range(2):
            onward(lambda to_t, child: down_z(part, to_t, child), sent)

    @pl.when((l == 0) & (t > 0))
    def _():
        each(layers - 1, lambda i: column_to(i + 1).wait_send())

        def other(i):
            to_t = 1 + lax.rem(t - 1 + i, tiles - 1)
            pl.when((to_t != t) | (t // span != 0))(lambda: other_to(to_t).wait_send())

        each(tiles - 1, other)


def emit_kernel(a, b, c, d, a_out, b_out, c_out, d_out, sems):
    copies = [
        pltpu.make_async_copy(src, dst, sems.at[i])
        for i, (src, dst) in enumerate(((a, a_out), (c, c_out), (b, b_out), (d, d_out)))
    ]
    for copy in copies:
        copy.start()
    for copy in copies:
        copy.wait()


def fixed(x):
    return pltpu.with_memory_space_constraint(x, pltpu.HBM)


def body(tiles, layers, basis, ranks, cores, diag):
    rmax = basis.shape[2]
    span = cores.shape[1]
    rows, order = diag.shape[1], diag.shape[2]
    panels = order // B
    vm = pl.BlockSpec(memory_space=pltpu.VMEM)
    hbm = pl.BlockSpec(memory_space=pl.ANY)
    f32 = jnp.float32
    dma = pltpu.SemaphoreType.DMA
    shapes = ((1, rows, order), (rmax, order), diag.shape, cores.shape)
    children = max(layers, tiles // 2)
    results = pl.pallas_call(
        functools.partial(panel_kernel, tiles, layers),
        out_shape=tuple(pltpu.VMEM(shape, f32) for shape in shapes),
        in_specs=[hbm, hbm, pl.BlockSpec(memory_space=pltpu.SMEM), hbm],
        out_specs=(vm,) * 4,
        scratch_shapes=[
            pltpu.VMEM((panels, order, B), f32),
            pltpu.VMEM((order, order), f32),
            pltpu.VMEM((B, B), f32),
            pltpu.VMEM((B, B), f32),
            pltpu.VMEM((B, B), f32),
            pltpu.VMEM((rmax, order), f32),
            pltpu.VMEM((rmax, rmax), f32),
            pltpu.VMEM((span, rmax, rmax), f32),
            pltpu.VMEM((order, rmax), f32),
            pltpu.VMEM((rmax, order), f32),
            pltpu.VMEM((rmax, rmax), f32),
            dma((3,)),
            dma((panels, layers)),
            dma((panels,)),
            dma((panels,)),
            dma((panels, children)),
            dma((2,)),
            dma((2, children)),
            dma,
            dma((layers,)),
            dma((span,)),
            dma((tiles,)),
        ],
        compiler_params=pltpu.CompilerParams(
            collective_id=0, has_side_effects=True, vmem_limit_bytes=24 << 20
        ),
    )(fixed(diag), fixed(basis[0].T), ranks, fixed(cores))
    factors, zt, schur, couplings = pl.pallas_call(
        emit_kernel,
        out_shape=tuple(jax.ShapeDtypeStruct(shape, f32) for shape in shapes),
        in_specs=[vm] * 4,
        out_specs=(hbm,) * 4,
        scratch_shapes=[dma((4,))],
        compiler_params=pltpu.CompilerParams(vmem_limit_bytes=1 << 20),
    )(*results)
    return factors, zt.T[None], schur, couplings


def solution(mesh):
    placed = (
        P("tile", None, None),
        P("tile"),
        P("tile", "layer", None, None),
        P("tile", "layer", None),
    )
    return jax.shard_map(
        functools.partial(body, mesh.shape["tile"], mesh.shape["layer"]),
        mesh=mesh,
        in_specs=placed,
        out_specs=(
            P(None, "layer", None),
            P(),
            P("tile", "layer", None),
            P("tile", "layer", None, None),
        ),
        check_vma=False,
    )
```

time: 59.5 us -> 46.1 us (0.77)
  the two profiles are of different devices: /device:TPU:11 before, /device:TPU:15 now
where the time goes in v1:
time: 46.1 us; the launch traced here: 45.9 us
  Pallas kernels  44.6 us (97%)
  between operations  1.28 us (3%)
    pallas_call x1, Pallas kernels, body(): pl.pallas_call(functools.partial(panel_kernel, tiles, layers), out_shape=...  43.6 us
    pallas_call x1, Pallas kernels, body(): pl.pallas_call(emit_kernel, out_shape=tuple((jax.ShapeDtypeStruct(shape,...  1.07 us

profile of v1, /device:TPU:15, one launch (start us, length us, event | category | flops | bytes accessed | tf_op | source)
XLA Modules:
  0.0 45.9 jit_solution(17490722566258504360)
XLA Ops:
  1.3 43.6 %shard_map.75 = (f32[1,192,768]{2,1,0:T(8,128)S(1)}, f32[32,768]{1,0:T(8,128)S(1)}, f32[1,192,768]{2,1,0:T(8,128)S(1)}, f32[1,2,32,32]{3,2,1,0:T(8,128)S(1)}) custom-call(f32[1,192,768]{2,1,0:T(8,128)} %diag_ref.1, f32[32,768]{1,0:T(8,128)} %bitcast.6, s32[1]{0:T(128)S(6)} %copy.8.ranks_ref, f32[1,2,32,32]{3,2,1,0:T(8,128)} %cores_ref.1), custom_call_target="tpu_custom_call" | custom-call | tf_op jit(solution)/shard_map/pallas_call | solution.py:462
  44.9 1.1 %shard_map.76 = (f32[1,192,768]{2,1,0:T(8,128)}, f32[32,768]{1,0:T(8,128)}, f32[1,192,768]{2,1,0:T(8,128)}, f32[1,2,32,32]{3,2,1,0:T(8,128)}) custom-call(f32[1,192,768]{2,1,0:T(8,128)S(1)} %get-tuple-element.12.a, f32[32,768]{1,0:T(8,128)S(1)} %get-tuple-element.13.b, f32[1,192,768]{2,1,0:T(8,128)S(1)} %get-tuple-element.14.c, ...), custom_call_target="tpu_custom_call" | custom-call | tf_op jit(solution)/shard_map/pallas_call | solution.py:495

commit v2 on v1

--- a/solution.py
+++ b/solution.py
@@ -36,6 +36,14 @@
 
 def tn(a, b):
     return three(a, b, ((0,), (0,)))
+
+
+def pair_nt(a, b):
+    (ah, al), (bh, bl) = a, b
+    dot = functools.partial(
+        lax.dot_general, dimension_numbers=(((1,), (1,)), ((), ())), preferred_element_type=jnp.float32
+    )
+    return dot(ah, bh) + dot(jnp.concatenate([ah, al], axis=1), jnp.concatenate([bl, bh], axis=1))
 
 
 def total(terms):
@@ -117,7 +125,7 @@
 def panel_kernel(
     tiles, layers, diag_ref, basis_ref, ranks_ref, cores_ref,
     factor_ref, z_ref, diag_out, cores_out,
-    work, low, block, upper, inverse, masked_t, col, oth, w_rows, w_cols, gram,
+    work, low, low_h, low_l, inv_h, inv_l, z_h, z_l, z_rest, corr, block, upper, inverse, masked_t, col, oth, w_rows, w_cols, gram,
     local, recv_work, send_work, recv_low, send_low, recv_z, send_z,
     recvc, sendc, recvo, sendo,
 ):
@@ -146,24 +154,28 @@
     def needed(j, piece):
         return (piece + 1) * rows > j * B
 
-    def columns(j):
-        return pl.ds(pl.multiple_of(j * B, B), B)
-
-    def slot(j, piece):
-        return work.at[j, pl.ds(pl.multiple_of(piece * rows, S), rows), :]
-
-    def gathered(j):
+    def parcels(piece):
+        top, end = piece * rows, (piece + 1) * rows
+        wide = min(2 * B, order)
+        cuts = [(0, B, 0, B), (B, 2 * B, 0, wide), (2 * B, 3 * B, 0, wide), (3 * B, order, 0, wide)]
+        cuts += [(j * B, order, j * B, j * B + B) for j in range(2, panels)]
+        found = []
+        for tag, (r0, r1, c0, c1) in enumerate(cuts):
+            r0, r1 = max(r0, top), min(r1, end)
+            if r0 < r1:
+                found.append((tag, r0, r1, c0, c1))
+        return found
+
+    def gathered(piece, tag, r0, r1, c0, c1):
         return remote(
-            diag_ref.at[0, :, columns(j)], slot(j, l), send_work.at[j], recv_work.at[j, l], 0, 0
+            diag_ref.at[0, r0 - piece * rows : r1 - piece * rows, c0:c1], work.at[r0:r1, c0:c1],
+            send_work.at[tag], recv_work.at[piece, tag], 0, 0,
         )
 
-    def kept(j):
+    def kept(tag, r0, r1, c0, c1):
         return pltpu.make_async_copy(
-            diag_ref.at[0, :, columns(j)], slot(j, 0), recv_work.at[j, 0]
+            diag_ref.at[0, r0:r1, c0:c1], work.at[r0:r1, c0:c1], recv_work.at[0, tag]
         )
-
-    def landed(j, piece):
-        return remote(slot(j, piece), slot(j, piece), send_work.at[j], recv_work.at[j, piece], t, l)
 
     def parts(k):
         whole, cut = (k * B) // rows, (k * B) % rows
@@ -182,15 +194,19 @@
             send_low.at[k, piece], recv_low.at[k], jnp.where(piece == 0, 1, 0), piece,
         )
 
+    edges = (0, panels // 2 * B, early, order)
+
+    def z_part(part):
+        return z_ref.at[:, edges[part] : edges[part + 1]]
+
     def out_z(part, piece):
-        cut = z_ref.at[:, early:] if part else z_ref.at[:, :early]
         return remote(
-            cut, cut, send_z.at[part, piece], recv_z.at[part], jnp.where(piece == 0, 1, 0), piece
+            z_part(part), z_part(part), send_z.at[part, piece], recv_z.at[part],
+            jnp.where(piece == 0, 1, 0), piece,
         )
 
     def down_z(part, to_t, child):
-        cut = z_ref.at[:, early:] if part else z_ref.at[:, :early]
-        return remote(cut, cut, send_z.at[part, child], recv_z.at[part], to_t, l)
+        return remote(z_part(part), z_part(part), send_z.at[part, child], recv_z.at[part], to_t, l)
 
     def onward(copy, act):
         @pl.when(fan)
@@ -235,7 +251,8 @@
 
     @pl.when(hub)
     def _():
-        each(panels, lambda j: pl.when(needed(j, 0))(lambda: kept(j).start()))
+        for parcel in parcels(0):
+            kept(*parcel).start()
         basis_in.start()
 
         def greet(i):
@@ -252,74 +269,147 @@
         pl.semaphore_signal(barrier, inc=1, device_id=(0, 0), device_id_type=pl.DeviceIdType.MESH)
         pl.semaphore_wait(barrier, 1)
 
-    def gather(j):
-        if 0 < j <= panels:
-            pl.when((t == 0) & spoke & needed(j - 1, l))(lambda: gathered(j - 1).wait_send())
-        if j < panels:
-            pl.when((t == 0) & spoke & needed(j, l))(lambda: gathered(j).start())
-
-    for j in range(3):
-        gather(j)
+    def gather(step):
+        for piece in range(1, layers):
+            moves = parcels(piece)
+            now = [(m, True) for m in moves[step : step + 1]]
+            if step > 1:
+                now = [(m, False) for m in moves[step - 2 : step - 1]] + now
+            if now:
+                @pl.when((t == 0) & (l == piece))
+                def _():
+                    for move, begin in now:
+                        copy = gathered(piece, *move)
+                        copy.start() if begin else copy.wait_send()
+
+    for step in range(4):
+        gather(step)
 
     diag_in.start()
     cores_in.start()
 
+    def land(piece, parcel):
+        if piece:
+            gathered(piece, *parcel).wait_recv()
+        else:
+            kept(*parcel).wait()
+
+    def arrived(tag, block_row=None):
+        for piece in range(layers):
+            for parcel in parcels(piece):
+                if parcel[0] != tag:
+                    continue
+                near = block_row is None or (
+                    piece * rows < (block_row + 1) * B and (piece + 1) * rows > block_row * B
+                )
+                yield near, functools.partial(land, piece, parcel)
+
+    def await_near(tag, block_row):
+        for near, wait in arrived(tag, block_row):
+            if near:
+                wait()
+
+    def await_far(tag, block_row):
+        for near, wait in arrived(tag, block_row):
+            if not near:
+                wait()
+
+    def await_all(tag):
+        for _, wait in arrived(tag):
+            wait()
+
+    def span_of(first, last):
+        return slice(first * B, last * B)
+
+    def halves(r, c):
+        return low_h[r, c], low_l[r, c]
+
+    def put(r, c, value):
+        low[r, c] = value
+        low_h[r, c], low_l[r, c] = split(value)
+
+    def inverse_of(k):
+        return inv_h[k], inv_l[k]
+
+    def catch_up(k, first, last):
+        r = span_of(first, last)
+        done, here = span_of(k - 1, k), span_of(k, k + 1)
+        put(r, done, pair_nt(split(work[r, done]), inverse_of(k - 1)))
+        before = span_of(0, k)
+        work[r, here] = work[r, here] - pair_nt(halves(r, before), halves(here, before))
+
+    def stage(k):
+        here, following = span_of(k, k + 1), span_of(k + 1, k + 2)
+        if k:
+            before = span_of(0, k)
+            z_rest[...] = masked_t[:, here] - pair_nt(
+                (z_h[:, before], z_l[:, before]), halves(here, before)
+            )
+            if k + 1 < panels:
+                catch_up(k, k + 1, k + 2 if k == 1 else panels)
+                corr[...] = pair_nt(halves(following, before), halves(following, before))
+        base_factor(block, upper, inverse)
+
+    def settle(k):
+        here, following = span_of(k, k + 1), span_of(k + 1, k + 2)
+        inv = split(inverse[...])
+        inv_h[k], inv_l[k] = inv
+        put(here, here, upper[...].T)
+        if k + 1 < panels:
+            below = pair_nt(split(work[following, here]), inv)
+            put(following, here, below)
+            parts_of = split(below)
+            rest = work[following, following] - pair_nt(parts_of, parts_of)
+            block[...] = rest - corr[...] if k else rest
+        part = z_rest[...] if k else masked_t[:, here]
+        solved = pair_nt(split(part), inv)
+        z_ref[:, here] = solved
+        z_h[:, here], z_l[:, here] = split(solved)
+
+    def ship_low(c):
+        for _, first, last, cut in parts(c):
+            for piece in range(first, last):
+                out_low(c, cut, piece).start()
+
+    def ship_z(part):
+        for piece in range(layers):
+            out_z(part, piece).start()
+
     @pl.when(hub)
     def _():
-        low[...] = jnp.zeros_like(low)
-
-        def panel(k, carry):
-            at = pl.ds(pl.multiple_of(k * B, B), B)
-
-            @pl.when(needed(k, 0))
-            def _():
-                kept(k).wait()
-
-            def take(piece):
-                pl.when(needed(k, piece + 1))(lambda: landed(k, piece + 1).wait_recv())
-
-            each(layers - 1, take)
-
-            for c in range(panels):
-                @pl.when(k == c)
-                def _():
-                    here = slice(c * B, c * B + B)
-                    if c:
-                        work2 = work[c, c * B :, :] - nt(low[c * B :, : c * B], low[here, : c * B])
-                        low[c * B :, here] = work2
-                    else:
-                        low[:, here] = work[0]
-            block[...] = low[at, at]
-
-            base_factor(block, upper, inverse)
-            low[at, at] = upper[...].T
-
-            @pl.when(k == 0)
-            def _():
+        await_all(0)
+        block[...] = work[:B, :B]
+        for k in range(panels):
+            if k == 1:
+                await_all(2)
+            if k > 1:
+                await_far(k + 2, k)
+            stage(k)
+            if k == 0:
                 mask()
+                await_all(1)
+            elif k + 1 < panels:
+                await_near(k + 3, k + 1)
+            settle(k)
+            if k == 1:
+                await_all(3)
+                catch_up(1, 3, panels)
                 pl.semaphore_wait(barrier, devices - 1)
-
-            for c in range(panels):
-                @pl.when(k == c)
-                def _():
-                    here = slice(c * B, c * B + B)
-                    rest = slice(c * B + B, order)
-                    if c + 1 < panels:
-                        low[rest, here] = nt(low[rest, here], inverse[...])
-                    part = masked_t[:, here]
-                    if c:
-                        part = part - nt(z_ref[:, : c * B], low[here, : c * B])
-                    z_ref[:, here] = nt(part, inverse[...])
-                    if c == panels - 1:
-                        each(layers, lambda piece: out_z(1, piece).start())
-                    for _, first, last, cut in parts(c):
-                        each(last - first, lambda i: out_low(c, cut, first + i).start())
-                    if c == panels - 2:
-                        each(layers, lambda piece: out_z(0, piece).start())
-            return carry
-
-        lax.fori_loop(0, panels, panel, 0)
-        factor_ref[0] = low[:rows, :]
+            if k == panels - 1:
+                ship_z(2)
+                ship_low(k)
+            elif k:
+                ship_low(k - 1)
+            if k == panels - 2:
+                ship_low(k)
+                ship_z(1)
+            if k == panels // 2 - 1:
+                ship_z(0)
+        factor_ref[...] = jnp.zeros_like(factor_ref)
+        for c in range(panels):
+            r0, r1 = c * B, min(rows, order)
+            if r0 < r1:
+                factor_ref[0, r0:r1, c * B : c * B + B] = low[r0:r1, c * B : c * B + B]
 
     @pl.when(spoke)
     def _():
@@ -332,7 +422,7 @@
                     down_low(k, cut, t, 0).wait_recv()
                     onward(lambda to_t, child: down_low(k, cut, to_t, child), start)
 
-            gather(k + 3)
+            gather(k + 4)
 
         relay(0)
 
@@ -374,14 +464,21 @@
             own = masked_t[...].T
             w_rows[...] = nn(own, col[...])
 
+        def relay_z(part):
+            down_z(part, t, 0).wait_recv()
+            onward(lambda to_t, child: down_z(part, to_t, child), start)
+
         for k in range(2, panels - 1):
+            if k == panels // 2 - 1:
+                relay_z(0)
             relay(k)
-        down_z(0, t, 0).wait_recv()
-        onward(lambda to_t, child: down_z(0, to_t, child), start)
+        relay_z(1)
         gram[...] = nt(z_ref[:, :early], z_ref[:, :early])
-        down_z(1, t, 0).wait_recv()
-        onward(lambda to_t, child: down_z(1, to_t, child), start)
+        relay_z(2)
         relay(panels - 1)
+
+        for step in range(panels + 4, panels + 8):
+            gather(step)
 
         @pl.when(t == 0)
         def _():
@@ -409,7 +506,7 @@
         for c in range(panels):
             for _, first, last, cut in parts(c):
                 each(last - first, lambda i: out_low(c, cut, first + i).wait_send())
-        for part in range(2):
+        for part in range(3):
             each(layers, lambda piece: out_z(part, piece).wait_send())
 
     @pl.when(spoke)
@@ -419,7 +516,7 @@
                 @pl.when(mine)
                 def _():
                     onward(lambda to_t, child: down_low(k, cut, to_t, child), sent)
-        for part in range(2):
+        for part in range(3):
             onward(lambda to_t, child: down_z(part, to_t, child), sent)
 
     @pl.when((l == 0) & (t > 0))
@@ -455,7 +552,7 @@
     panels = order // B
     vm = pl.BlockSpec(memory_space=pltpu.VMEM)
     hbm = pl.BlockSpec(memory_space=pl.ANY)
-    f32 = jnp.float32
+    f32, bf16 = jnp.float32, jnp.bfloat16
     dma = pltpu.SemaphoreType.DMA
     shapes = ((1, rows, order), (rmax, order), diag.shape, cores.shape)
     children = max(layers, tiles // 2)
@@ -465,8 +562,16 @@
         in_specs=[hbm, hbm, pl.BlockSpec(memory_space=pltpu.SMEM), hbm],
         out_specs=(vm,) * 4,
         scratch_shapes=[
-            pltpu.VMEM((panels, order, B), f32),
             pltpu.VMEM((order, order), f32),
+            pltpu.VMEM((order, order), f32),
+            pltpu.VMEM((order, order), bf16),
+            pltpu.VMEM((order, order), bf16),
+            pltpu.VMEM((panels, B, B), bf16),
+            pltpu.VMEM((panels, B, B), bf16),
+            pltpu.VMEM((rmax, order), bf16),
+            pltpu.VMEM((rmax, order), bf16),
+            pltpu.VMEM((rmax, B), f32),
+            pltpu.VMEM((B, B), f32),
             pltpu.VMEM((B, B), f32),
             pltpu.VMEM((B, B), f32),
             pltpu.VMEM((B, B), f32),
@@ -477,12 +582,12 @@
             pltpu.VMEM((rmax, order), f32),
             pltpu.VMEM((rmax, rmax), f32),
             dma((3,)),
-            dma((panels, layers)),
-            dma((panels,)),
+            dma((layers, panels + 2)),
+            dma((panels + 2,)),
             dma((panels,)),
             dma((panels, children)),
-            dma((2,)),
-            dma((2, children)),
+            dma((3,)),
+            dma((3, children)),
             dma,
             dma((layers,)),
             dma((span,)),

time: 46.1 us -> 45.2 us (0.980)
  Pallas kernels: 44.6 us -> 43.8 us
    pallas_call x1, Pallas kernels: 43.6 us -> 42.7 us  [body(): pl.pallas_call(functools.partial(panel_kernel, tiles, layers), out_shape=...]
where the time goes in v2:
time: 45.2 us; the launch traced here: 45.1 us
  Pallas kernels  43.8 us (97%)
  between operations  1.28 us (3%)
    pallas_call x1, Pallas kernels, body(): pl.pallas_call(functools.partial(panel_kernel, tiles, layers), out_shape=...  42.7 us
    pallas_call x1, Pallas kernels, body(): pl.pallas_call(emit_kernel, out_shape=tuple((jax.ShapeDtypeStruct(shape,...  1.07 us

profile of v2, /device:TPU:15, one launch (start us, length us, event | category | flops | bytes accessed | tf_op | source)
XLA Modules:
  0.0 45.1 jit_solution(5183444411591462333)
XLA Ops:
  1.3 42.7 %shard_map.75 = (f32[1,192,768]{2,1,0:T(8,128)S(1)}, f32[32,768]{1,0:T(8,128)S(1)}, f32[1,192,768]{2,1,0:T(8,128)S(1)}, f32[1,2,32,32]{3,2,1,0:T(8,128)S(1)}) custom-call(f32[1,192,768]{2,1,0:T(8,128)} %diag_ref.1, f32[32,768]{1,0:T(8,128)} %bitcast.6, s32[1]{0:T(128)S(6)} %copy.8.ranks_ref, f32[1,2,32,32]{3,2,1,0:T(8,128)} %cores_ref.1), custom_call_target="tpu_custom_call" | custom-call | tf_op jit(solution)/shard_map/pallas_call | solution.py:559
  44.0 1.1 %shard_map.76 = (f32[1,192,768]{2,1,0:T(8,128)}, f32[32,768]{1,0:T(8,128)}, f32[1,192,768]{2,1,0:T(8,128)}, f32[1,2,32,32]{3,2,1,0:T(8,128)}) custom-call(f32[1,192,768]{2,1,0:T(8,128)S(1)} %get-tuple-element.12.a, f32[32,768]{1,0:T(8,128)S(1)} %get-tuple-element.13.b, f32[1,192,768]{2,1,0:T(8,128)S(1)} %get-tuple-element.14.c, ...), custom_call_target="tpu_custom_call" | custom-call | tf_op jit(solution)/shard_map/pallas_call | solution.py:600
